TPU v7x, 32 devices: a whole 2x2x4 slice. The times are simulated.
32 devices in a mesh: fsdp: 4 (over y, x), seq: 8 (over z, core).
Axes of the slice: x: 2, y: 2, z: 4, core: 2. Of those that a mesh axis runs over, the one named last changes fastest.
Arguments:
- block_input: float32 [4, 1024, 1024], P('fsdp', 'seq'), may hold values from -6 to 6
- norm_gain: float32 [1024], replicated, may hold values from 0.5 to 1.5
- w_in: bfloat16 [1024, 4384], P('fsdp', 'seq'), may hold values from -0.1875 to 0.1875
- conv_w: float32 [4, 2304], replicated, may hold values from -0.5 to 0.5
- conv_b: float32 [2304], replicated, may hold values from -0.5 to 0.5
- dt_bias: float32 [32], replicated, may hold values from -6.5 to -2.5
- a_log: float32 [32], replicated, may hold values from 0 to 2.77
- skip_gain: float32 [32], replicated, may hold values from 0.5 to 1.5
- gate_gain: float32 [2048], replicated, may hold values from 0.5 to 1.5
- w_out: bfloat16 [2048, 1024], P('fsdp', 'seq'), may hold values from -0.125 to 0.125
- out_cotangent: float32 [4, 1024, 1024], P('fsdp', 'seq'), may hold values from -6 to 6
Outputs:
- block_output: float32 [4, 1024, 1024], P('fsdp', 'seq')
- grad_input: float32 [4, 1024, 1024], P('fsdp', 'seq')
- grad_norm_gain: float32 [1024], replicated
- grad_w_in: float32 [1024, 4384], P('fsdp', 'seq')
- grad_conv_w: float32 [4, 2304], replicated
- grad_conv_b: float32 [2304], replicated
- grad_dt_bias: float32 [32], replicated
- grad_a_log: float32 [32], replicated
- grad_skip_gain: float32 [32], replicated
- grad_gate_gain: float32 [2048], replicated
- grad_w_out: float32 [2048, 1024], P('fsdp', 'seq')
All inputs are finite; a program needn't handle non-finite values.
Results may differ from a plain program's by a relative error of at most 0.011.
Values may be sent and summed in bfloat16 or wider, within the bound.
No kernel may reach another device: no remote copies, remote signals or barrier semaphores. Data moves between devices by JAX's collectives and lax.ppermute only.
A program may use at most 128 MiB of HBM per device.

v0:
```python
import jax
import jax.numpy as jnp
from jax import lax
from jax.sharding import PartitionSpec as P

DI = 2048
HEADS = 32
HEAD_DIM = 64
STATE = 128
CONV_W = 4
GROUP = 128
EPS = 1e-05


def rms_apply(values, norm_gain):
    return values * lax.rsqrt(jnp.mean(values * values, axis=-1, keepdims=True) + EPS) * norm_gain


def gated_apply(values, gate_values, norm_gain):
    return rms_apply(values * jax.nn.silu(gate_values), norm_gain)


def causal_conv(signal, kernel, offset):
    taps = kernel.shape[0]
    length = signal.shape[0]
    padded = jnp.pad(signal, ((taps - 1, 0), (0, 0)))
    summed = offset + kernel[0] * padded[0:length]
    for tap_index in range(1, taps):
        summed = summed + kernel[tap_index] * padded[tap_index : tap_index + length]
    return jax.nn.silu(summed)


def state_space(signal, step_size, b_rows, c_rows, log_rate, skip_value):
    length = signal.shape[0]
    channels = signal.shape[1]
    blocks = length // GROUP
    highest = lax.Precision.HIGHEST
    decay_rate = -jnp.exp(log_rate) * step_size
    x_blocks = signal.reshape(blocks, GROUP, channels)
    step_blocks = step_size.reshape(blocks, GROUP)
    b_blocks = b_rows.reshape(blocks, GROUP, b_rows.shape[1])
    c_blocks = c_rows.reshape(blocks, GROUP, c_rows.shape[1])
    running = jnp.cumsum(decay_rate.reshape(blocks, GROUP), axis=1)
    scores = jnp.einsum("cin,cjn->cij", c_blocks, b_blocks, precision=highest)
    row_index = lax.broadcasted_iota(jnp.int32, (GROUP, GROUP), 0)
    col_index = lax.broadcasted_iota(jnp.int32, (GROUP, GROUP), 1)
    causal = row_index >= col_index
    spread = running[:, :, None] - running[:, None, :]
    decay = jnp.where(causal, jnp.exp(jnp.where(causal, spread, 0.0)), 0.0)
    within = jnp.einsum(
        "cij,cjp->cip", scores * decay * step_blocks[:, None, :], x_blocks, precision=highest
    )
    toward = jnp.exp(running[:, -1:] - running) * step_blocks
    inflow = jnp.einsum("cjp,cjn->cpn", x_blocks * toward[:, :, None], b_blocks, precision=highest)
    carried = jnp.exp(running[:, -1])

    def advance(memory, packet):
        factor, update = packet
        return (factor * memory + update, memory)

    _, openings = lax.scan(
        advance, jnp.zeros((channels, b_rows.shape[1]), signal.dtype), (carried, inflow)
    )
    across = jnp.exp(running)[:, :, None] * jnp.einsum(
        "cin,cpn->cip", c_blocks, openings, precision=highest
    )
    return (within + across).reshape(length, channels) + skip_value * signal


def mixer_head(
    x_raw,
    dt_raw,
    b_raw,
    c_raw,
    kern_x,
    bias_x,
    kern_b,
    bias_b,
    kern_c,
    bias_c,
    log_rate,
    skip_value,
    dt_shift,
):
    x_act = causal_conv(x_raw, kern_x, bias_x)
    b_act = causal_conv(b_raw, kern_b, bias_b)
    c_act = causal_conv(c_raw, kern_c, bias_c)
    step_size = jax.nn.softplus(dt_raw + dt_shift)
    return state_space(x_act, step_size, b_act, c_act, log_rate, skip_value)


def inner_rows(left, right):
    return lax.dot_general(
        left, right, (((0,), (0,)), ((), ())), preferred_element_type=jnp.float32
    )


def outer_cols(left, right):
    return lax.dot_general(
        left, right, (((1,), (1,)), ((), ())), preferred_element_type=jnp.float32
    )


def per_device(
    block_input,
    norm_gain,
    w_in,
    conv_w,
    conv_b,
    dt_bias,
    a_log,
    skip_gain,
    gate_gain,
    w_out,
    out_cotangent,
):
    residual = block_input[0]
    grad_out = out_cotangent[0]
    tokens = residual.shape[0]
    in_columns, out_columns = (
        lax.all_gather(w_in, "seq", axis=1, tiled=True),
        lax.all_gather(w_out, "seq", axis=1, tiled=True),
    )
    w_in_full, w_out_full = (
        lax.all_gather(in_columns, "fsdp", axis=0, tiled=True),
        lax.all_gather(out_columns, "fsdp", axis=0, tiled=True),
    )
    normed, norm_pull = jax.vjp(rms_apply, residual, norm_gain)
    normed_half = normed.astype(jnp.bfloat16)
    projected = jnp.dot(normed_half, w_in_full, preferred_element_type=jnp.float32).astype(
        jnp.bfloat16
    )
    gate_half = projected[:, :DI]
    inner_part = projected[:, DI : 2 * DI].reshape(tokens, HEADS, HEAD_DIM)
    step_part = projected[:, 2 * DI + 2 * STATE :]
    inner_heads, step_heads = (
        lax.all_to_all(inner_part, "seq", split_axis=1, concat_axis=0, tiled=True),
        lax.all_to_all(step_part, "seq", split_axis=1, concat_axis=0, tiled=True),
    )
    input_rows, output_rows = (
        lax.all_gather(projected[:, 2 * DI : 2 * DI + STATE], "seq", axis=0, tiled=True),
        lax.all_gather(
            projected[:, 2 * DI + STATE : 2 * DI + 2 * STATE], "seq", axis=0, tiled=True
        ),
    )
    local_heads = inner_heads.shape[1]
    head_start = lax.axis_index("seq") * local_heads
    kern_x = lax.dynamic_slice_in_dim(
        conv_w[:, :DI].reshape(CONV_W, HEADS, HEAD_DIM), head_start, local_heads, 1
    )
    bias_x = lax.dynamic_slice_in_dim(
        conv_b[:DI].reshape(HEADS, HEAD_DIM), head_start, local_heads, 0
    )
    kern_b = conv_w[:, DI : DI + STATE]
    kern_c = conv_w[:, DI + STATE :]
    bias_b = conv_b[DI : DI + STATE]
    bias_c = conv_b[DI + STATE :]
    rate_local = lax.dynamic_slice_in_dim(a_log, head_start, local_heads, 0)
    skip_local = lax.dynamic_slice_in_dim(skip_gain, head_start, local_heads, 0)
    shift_local = lax.dynamic_slice_in_dim(dt_bias, head_start, local_heads, 0)
    mixer_many = jax.vmap(
        mixer_head, in_axes=(1, 1, None, None, 1, 0, None, None, None, None, 0, 0, 0), out_axes=1
    )
    y_heads, mixer_pull = jax.vjp(
        mixer_many,
        inner_heads.astype(jnp.float32),
        step_heads.astype(jnp.float32),
        input_rows.astype(jnp.float32),
        output_rows.astype(jnp.float32),
        kern_x,
        bias_x,
        kern_b,
        bias_b,
        kern_c,
        bias_c,
        rate_local,
        skip_local,
        shift_local,
    )
    y_tokens = lax.all_to_all(
        y_heads.astype(jnp.bfloat16), "seq", split_axis=0, concat_axis=1, tiled=True
    ).reshape(tokens, DI)
    gated, gate_pull = jax.vjp(
        gated_apply, y_tokens.astype(jnp.float32), gate_half.astype(jnp.float32), gate_gain
    )
    gated_half = gated.astype(jnp.bfloat16)
    block_out = residual + jnp.dot(gated_half, w_out_full, preferred_element_type=jnp.float32)
    cot_half = grad_out.astype(jnp.bfloat16)
    w_in_back, w_out_back = (w_in_full, w_out_full)
    g_w_out = inner_rows(gated_half, cot_half)
    dgated = outer_cols(cot_half, w_out_back)
    grad_y, grad_z, g_gate = gate_pull(dgated)
    dy_heads = lax.all_to_all(
        grad_y.astype(jnp.bfloat16).reshape(tokens, HEADS, HEAD_DIM),
        "seq",
        split_axis=1,
        concat_axis=0,
        tiled=True,
    )
    pieces = mixer_pull(dy_heads.astype(jnp.float32))
    g_xr, g_dtr, g_br, g_cr, g_kx, g_bx, g_kb, g_bb, g_kc, g_bc, g_rate, g_skip, g_shift = pieces
    dx_tokens, ddt_tokens = (
        lax.all_to_all(g_xr.astype(jnp.bfloat16), "seq", split_axis=0, concat_axis=1, tiled=True),
        lax.all_to_all(g_dtr.astype(jnp.bfloat16), "seq", split_axis=0, concat_axis=1, tiled=True),
    )
    db_tokens, dc_tokens = (
        lax.psum_scatter(g_br, "seq", scatter_dimension=0, tiled=True),
        lax.psum_scatter(g_cr, "seq", scatter_dimension=0, tiled=True),
    )
    dproj = jnp.concatenate(
        [
            grad_z.astype(jnp.bfloat16),
            dx_tokens.reshape(tokens, DI),
            db_tokens.astype(jnp.bfloat16),
            dc_tokens.astype(jnp.bfloat16),
            ddt_tokens,
        ],
        axis=1,
    )
    g_w_in = inner_rows(normed_half, dproj)
    dnormed = outer_cols(dproj, w_in_back)
    du_norm, g_norm = norm_pull(dnormed)
    grad_in = grad_out + du_norm
    rows_in, rows_out = (
        lax.psum_scatter(g_w_in, "fsdp", scatter_dimension=0, tiled=True),
        lax.psum_scatter(g_w_out, "fsdp", scatter_dimension=0, tiled=True),
    )
    owned_w_in, owned_w_out = (
        lax.psum_scatter(rows_in, "seq", scatter_dimension=1, tiled=True),
        lax.psum_scatter(rows_out, "seq", scatter_dimension=1, tiled=True),
    )
    kern_full = lax.dynamic_update_slice_in_dim(
        jnp.zeros((CONV_W, HEADS, HEAD_DIM), jnp.float32), g_kx, head_start, 1
    ).reshape(CONV_W, DI)
    g_conv_w = jnp.concatenate([kern_full, g_kb, g_kc], axis=1)
    offset_full = lax.dynamic_update_slice_in_dim(
        jnp.zeros((HEADS, HEAD_DIM), jnp.float32), g_bx, head_start, 0
    ).reshape(DI)
    g_conv_b = jnp.concatenate([offset_full, g_bb, g_bc])
    shift_full = lax.dynamic_update_slice_in_dim(
        jnp.zeros((HEADS,), jnp.float32), g_shift, head_start, 0
    )
    rate_full = lax.dynamic_update_slice_in_dim(
        jnp.zeros((HEADS,), jnp.float32), g_rate, head_start, 0
    )
    skip_full = lax.dynamic_update_slice_in_dim(
        jnp.zeros((HEADS,), jnp.float32), g_skip, head_start, 0
    )
    summed = lax.psum(
        (g_norm, g_conv_w, g_conv_b, shift_full, rate_full, skip_full, g_gate), ("fsdp", "seq")
    )
    return (
        block_out[None],
        grad_in[None],
        summed[0],
        owned_w_in,
        summed[1],
        summed[2],
        summed[3],
        summed[4],
        summed[5],
        summed[6],
        owned_w_out,
    )


def solution(mesh):
    return jax.shard_map(
        per_device,
        mesh=mesh,
        in_specs=(
            P("fsdp", "seq", None),
            P(),
            P("fsdp", "seq"),
            P(),
            P(),
            P(),
            P(),
            P(),
            P(),
            P("fsdp", "seq"),
            P("fsdp", "seq", None),
        ),
        out_specs=(
            P("fsdp", "seq", None),
            P("fsdp", "seq", None),
            P(),
            P("fsdp", "seq"),
            P(),
            P(),
            P(),
            P(),
            P(),
            P(),
            P("fsdp", "seq"),
        ),
        check_vma=False,
    )
```

profile of v0, /device:TPU:0, one launch (start us, length us, event | category | flops | bytes accessed | tf_op | source)
XLA Modules:
  0.0 822.4 jit_solution(4524585330081583033)
XLA Ops:
  8.7 34.2 %all-gather.12.cloned.1.call-done = bf16[8,548,256]{2,1,0:T(8,128)(2,1)} async-done(((bf16[1,548,256]{2,1,0:T(8,128)(2,1)}), bf16[8,548,256]{2,1,0:T(8,128)(2,1)}) %all-gather.12.cloned.1.call-update) | async-done | bytes 2244624 | tf_op jit(solution)/shard_map/all_gather | solution.py:121
  50.7 17.1 %all-gather.8.cloned.1.call-done = bf16[512,1024]{1,0:T(8,128)(2,1)} async-done(((bf16[512,128]{1,0:T(8,128)(2,1)}), bf16[512,1024]{1,0:T(8,128)(2,1)}) %all-gather.8.cloned.1.call-update) | async-done | bytes 1048592 | tf_op jit(solution)/shard_map/all_gather | solution.py:122
  67.8 92.8 %all-gather.6.cloned.1.call-done = bf16[1024,4384]{0,1:T(8,128)(2,1)} async-done(((bf16[256,4384]{0,1:T(8,128)(2,1)}), bf16[1024,4384]{0,1:T(8,128)(2,1)}) %all-gather.6.cloned.1.call-update) | async-done | bytes 8978448 | tf_op jit(solution)/shard_map/all_gather | solution.py:125
  160.7 6.1 convolution_convert_fusion
  167.5 4.6 all-to-all-start
  172.1 13.6 %all_gather.21 = bf16[1024,128]{0,1:T(8,128)(2,1)S(1)} all-gather(bf16[128,128]{0,1:T(8,128)(2,1)S(1)} %get-tuple-element.340), channel_id=1, replica_groups=mesh['fsdp'=4,'seq'=8] {'seq'}, dimensions={0}, use_global_device_ids=true | all-gather | bytes 294912 | tf_op jit(solution)/shard_map/all_gather | solution.py:141
  185.8 13.1 %all_gather.20 = bf16[1024,128]{0,1:T(8,128)(2,1)S(1)} all-gather(bf16[128,128]{0,1:T(8,128)(2,1)S(1)} %get-tuple-element.339), channel_id=1, replica_groups=mesh['fsdp'=4,'seq'=8] {'seq'}, dimensions={0}, use_global_device_ids=true | all-gather | bytes 294912 | tf_op jit(solution)/shard_map/all_gather | solution.py:142
  205.9 4.7 all-to-all-start.1
  218.3 7.6 all-to-all-done.1
  232.3 23.3 %while.34 = (s32[]{:T(128)}, f32[4,64,128]{2,1,0:T(8,128)S(1)}, f32[8,4,64,128]{3,2,1,0:T(8,128)S(1)}, f32[8,4,1,1]{1,3,2,0:T(1,128)}, f32[8,4]{1,0:T(8,128)}, /...) while((s32[]{:T(128)}, f32[4,64,128]{2,1,0:T(8,128)S(1)}, f32[8,4,64,128]{3,2,1,0:T(8,128)S(1)}, ...), condition=%wide.region_3.4_spmd.clone, body=%wide.region_2.3_spmd.clone.sunk | while | flops 131075 | bytes 656552 | solution.py:61
  265.8 19.6 %all_to_all.83 = bf16[8,2,16384]{2,1,0:T(2,128)(2,1)} all-to-all(bf16[8,2,16384]{2,1,0:T(2,128)(2,1)} %reshape.324), channel_id=1, replica_groups=mesh['fsdp'=4,'seq'=8] {'seq'}, dimensions={0} | all-to-all | bytes 1048576 | tf_op jit(solution)/shard_map/all_to_all | solution.py:180
  304.9 15.3 %all-to-all-done.3 = bf16[128,32,64]{0,2,1:T(8,128)(2,1)} async-done(((bf16[128,32,64]{0,2,1:T(8,128)(2,1)}), bf16[128,32,64]{0,2,1:T(8,128)(2,1)}, u32[]{:S(2)}, u32[]{:S(2)}) %all-to-all-start.3) | async-done | bytes 524320 | tf_op jit(solution)/shard_map/all_to_all | solution.py:193
  321.5 5.2 fusion.18
  334.5 34.1 %while.35 = (s32[]{:T(128)}, f32[4,64,128]{2,1,0:T(8,128)S(1)}, f32[8,4]{1,0:T(8,128)}, f32[8,4,64,128]{3,2,1,0:T(8,128)}, f32[8,4,64,128]{3,2,1,0:T(8,128)}, /*...) while((s32[]{:T(128)}, f32[4,64,128]{2,1,0:T(8,128)S(1)}, ...), condition=%wide.region_8.9_spmd.clone, body=%wide.region_6.8_spmd.clone.sunk | while | flops 196608 | bytes 786676 | solution.py:61
  379.7 5.1 multiply_reduce_fusion.10
  409.4 5.0 reduce_window_sum.23
  415.2 8.1 all-to-all-done.4
  431.1 16.9 %reduce-scatter.10.cloned.1.call-done = f32[128,128]{0,1:T(8,128)} async-done(((f32[1024,128]{0,1:T(8,128)}), f32[128,128]{0,1:T(8,128)}) %reduce-scatter.10.cloned.1.call-update) | async-done | bytes 65552 | tf_op jit(solution)/shard_map/reduce_scatter | solution.py:208
  448.9 9.2 %fusion.92 = f32[1024,4384]{0,1:T(8,128)} fusion(bf16[128,4384]{0,1:T(8,128)(2,1)S(1)} %constant_dynamic-update-slice_fusion.1, f32[1,128,1024]{2,1,0:T(8,128)S(1)} %copy-done, f32[1024]{0:T(1024)S(1)} %copy-done.36, f32[128]{0:T(128)S(1)} %copy-done.60), kind=kOutput, calls=%fused_computation.241 | convolution fusion | flops 1149632512 | bytes 19608064 | tf_op jit(solution)/shard_map/dot_general | solution.py:93
  465.3 5.3 multiply_reduce_fusion.16
  470.7 64.6 %reduce-scatter.14.cloned.1.call-done = f32[512,1024]{1,0:T(8,128)} async-done(((f32[2048,1024]{1,0:T(8,128)}), f32[512,1024]{1,0:T(8,128)}) %reduce-scatter.14.cloned.1.call-update) | async-done | bytes 2097168 | tf_op jit(solution)/shard_map/reduce_scatter | solution.py:226
  535.3 166.4 %reduce-scatter.12.cloned.1.call-done = f32[256,4384]{0,1:T(8,128)} async-done(((f32[1024,4384]{0,1:T(8,128)}), f32[256,4384]{0,1:T(8,128)}) %reduce-scatter.12.cloned.1.call-update) | async-done | bytes 4489232 | tf_op jit(solution)/shard_map/reduce_scatter | solution.py:225
  701.7 70.2 %fusion = f32[256,552]{0,1:T(8,128)S(1)} fusion(f32[256,4384]{0,1:T(8,128)} %reduce-scatter.12.cloned.1.call-done), kind=kCustom, calls=%all-reduce-scatter | all-reduce-scatter fusion | flops 1130497 | bytes 5054976
  774.3 39.7 %all-reduce.31 = (f32[1024]{0:T(1024)}, f32[4,2304]{1,0:T(4,128)}, f32[2304]{0:T(1024)}, f32[32]{0:T(128)}, f32[32]{0:T(128)}, /*index=5*/f32[32]{0:T(128)}, f32[2048]{0:T(1024)}) all-reduce(f32[1024]{0:T(1024)S(1)} %get-tuple-element.282, f32[4,2304]{1,0:T(4,128)S(1)} %pad_maximum_fusion, ...), channel_id=1, replica_groups=mesh['fsdp'=4,'seq'=8] {'fsdp','seq'}, use_global_device_ids=true, to_apply=%region_21.22 | all-reduce | flops 14688 | bytes 117504 | tf_op jit(solution)/shard_map/psum | solution.py:249
  (417 shorter events, 181.3 us)
Async XLA Ops:
  7.2 35.7 %all-gather.12.cloned.1.call-start = ((), (), s32[]{:S(2)}) async-start(), calls=%async_computation.19 | async-start | bytes 2543616 | tf_op jit(solution)/shard_map/all_gather | solution.py:121
  7.9 59.9 %all-gather.8.cloned.1.call-start = ((), (), s32[]{:S(2)}) async-start(), calls=%async_computation.12 | async-start | bytes 1179648 | tf_op jit(solution)/shard_map/all_gather | solution.py:122
  8.7 152.0 %all-gather.6.cloned.1.call-start = ((), (), s32[]{:S(2)}) async-start(), calls=%async_computation.11 | async-start | bytes 11223040 | tf_op jit(solution)/shard_map/all_gather | solution.py:125
  47.0 246.5 %all-gather.10.cloned.1.call-start = ((), (), s32[]{:S(2)}) async-start(), calls=%async_computation.13 | async-start | bytes 5242880 | tf_op jit(solution)/shard_map/all_gather | solution.py:126
  47.9 167.0 %copy-start.79 = (f32[4]{0:T(128)}, f32[4]{0:T(128)S(1)}, u32[]{:S(2)}) copy-start(f32[4]{0:T(128)S(1)} %dynamic_slice.52) | copy-start | bytes 52
  48.6 166.3 %copy-start.81 = (f32[4]{0:T(128)}, f32[4]{0:T(128)S(1)}, u32[]{:S(2)}) copy-start(f32[4]{0:T(128)S(1)} %fusion.87) | copy-start | bytes 52
  50.6 148.4 %copy-start.71 = (f32[128]{0:T(128)}, f32[128]{0:T(128)S(1)}, u32[]{:S(2)}) copy-start(f32[128]{0:T(128)S(1)} %get-tuple-element.363) | copy-start | bytes 1540
  50.6 148.4 %copy-start.73 = (f32[128]{0:T(128)}, f32[128]{0:T(128)S(1)}, u32[]{:S(2)}) copy-start(f32[128]{0:T(128)S(1)} %get-tuple-element.364) | copy-start | bytes 1540
  50.6 149.8 %copy-start.63 = (f32[128]{0:T(128)}, f32[128]{0:T(128)S(1)}, u32[]{:S(2)}) copy-start(f32[128]{0:T(128)S(1)} %get-tuple-element.362) | copy-start | bytes 1540
  50.6 149.8 %copy-start.65 = (f32[128]{0:T(128)}, f32[128]{0:T(128)S(1)}, u32[]{:S(2)}) copy-start(f32[128]{0:T(128)S(1)} %get-tuple-element.366) | copy-start | bytes 1540
  50.6 149.8 %copy-start.67 = (f32[128]{0:T(128)}, f32[128]{0:T(128)S(1)}, u32[]{:S(2)}) copy-start(f32[128]{0:T(128)S(1)} %get-tuple-element.367) | copy-start | bytes 1540
  50.6 149.8 %copy-start.69 = (f32[128]{0:T(128)}, f32[128]{0:T(128)S(1)}, u32[]{:S(2)}) copy-start(f32[128]{0:T(128)S(1)} %get-tuple-element.368) | copy-start | bytes 1540
  167.5 38.4 %all-to-all-start = ((bf16[128,8,4]{0,2,1:T(4,128)(2,1)}), bf16[128,8,4]{0,2,1:T(4,128)(2,1)S(1)}, u32[]{:S(2)}, u32[]{:S(2)}) async-start(bf16[128,8,4]{0,2,1:T(4,128)(2,1)} %bitcast.12), calls=%async_computation | async-start | bytes 16384 | tf_op jit(solution)/shard_map/all_to_all | solution.py:138
  205.9 20.0 %all-to-all-start.1 = ((bf16[128,32,64]{0,2,1:T(8,128)(2,1)}), bf16[128,32,64]{0,2,1:T(8,128)(2,1)}, u32[]{:S(2)}, u32[]{:S(2)}) async-start(bf16[128,32,64]{0,2,1:T(8,128)(2,1)} %bitcast.444), calls=%async_computation.1 | async-start | bytes 1048576 | tf_op jit(solution)/shard_map/all_to_all | solution.py:137
  300.7 19.5 %all-to-all-start.3 = ((bf16[128,32,64]{0,2,1:T(8,128)(2,1)}), bf16[128,32,64]{0,2,1:T(8,128)(2,1)}, u32[]{:S(2)}, u32[]{:S(2)}) async-start(bf16[128,32,64]{0,2,1:T(8,128)(2,1)} %bitcast.447), calls=%async_computation.3 | async-start | bytes 1048576 | tf_op jit(solution)/shard_map/all_to_all | solution.py:193
  304.9 125.4 %reduce-scatter.8.cloned.1.call-start = ((), (), s32[]{:S(2)}) async-start(), calls=%async_computation.14 | async-start | bytes 589824 | tf_op jit(solution)/shard_map/reduce_scatter | solution.py:207
  386.4 61.7 %reduce-scatter.10.cloned.1.call-start = ((), (), s32[]{:S(2)}) async-start(), calls=%async_computation.15 | async-start | bytes 589824 | tf_op jit(solution)/shard_map/reduce_scatter | solution.py:208
  388.0 147.3 %reduce-scatter.14.cloned.1.call-start = ((), (), s32[]{:S(2)}) async-start(), calls=%async_computation.17 | async-start | bytes 10485760 | tf_op jit(solution)/shard_map/reduce_scatter | solution.py:226
  404.2 19.1 %all-to-all-start.4 = ((bf16[8,2,16384]{2,1,0:T(2,128)(2,1)}), bf16[8,2,16384]{2,1,0:T(2,128)(2,1)S(1)}, u32[]{:S(2)}, u32[]{:S(2)}) async-start(bf16[8,2,16384]{2,1,0:T(2,128)(2,1)} %reshape.326), calls=%async_computation.4 | async-start | bytes 1048576 | tf_op jit(solution)/shard_map/all_to_all | solution.py:203
  423.3 25.6 %all-to-all-start.5 = ((bf16[8,128,4]{1,2,0:T(4,128)(2,1)}), bf16[8,128,4]{1,2,0:T(4,128)(2,1)S(1)}, u32[]{:S(2)}, u32[]{:S(2)}) async-start(bf16[8,128,4]{1,2,0:T(4,128)(2,1)} %bitcast.385), calls=%async_computation.7 | async-start | bytes 16384 | tf_op jit(solution)/shard_map/all_to_all | solution.py:204
  426.6 275.1 %reduce-scatter.12.cloned.1.call-start = ((), (), s32[]{:S(2)}) async-start(), calls=%async_computation.16 | async-start | bytes 22446080 | tf_op jit(solution)/shard_map/reduce_scatter | solution.py:225
  458.1 357.3 %reduce-scatter.16.cloned.1.call-start = ((), (), s32[]{:S(2)}) async-start(), calls=%async_computation.18 | async-start | bytes 2359296 | tf_op jit(solution)/shard_map/reduce_scatter | solution.py:230
  535.3 238.0 %copy-start.15 = (f32[1,128,1024]{2,1,0:T(8,128)S(1)}, f32[1,128,1024]{2,1,0:T(8,128)}, u32[]{:S(2)}) copy-start(f32[1,128,1024]{2,1,0:T(8,128)} %param.25) | copy-start | bytes 1572868
  772.0 42.0 %collective-permute-start = (f32[256,28]{0,1:T(8,128)S(1)}, f32[256,28]{0,1:T(8,128)S(1)}, u32[]{:S(2)}, u32[]{:S(2)}) collective-permute-start(f32[256,28]{0,1:T(8,128)S(1)} %slice.156), channel_id=1, source_target_pairs={{0,1},{1,2},{2,3},{3,4},{4,5},{5,6},{6,7},{8,9},{9,10},{10,11},{11... | collective-permute-start | bytes 86024
  (95 other events, 1122.3 us)
Sparse Core Ops, SparseCore 0:
  9.6 33.2 all-gather.11
  44.5 23.2 all-gather.7
  69.6 90.9 all-gather.5
  162.3 52.5 all-gather.9
  386.5 29.5 reduce-scatter.7
  418.2 29.7 reduce-scatter.9
  451.1 84.1 reduce-scatter.13
  538.4 163.2 reduce-scatter.11
  704.6 50.0 reduce-scatter.15
where the time goes:
time: 830 us; the launch traced here: 822 us
  waiting for transfers between devices  425 us (51%)
  blocking collectives  156 us (19%)
  local copies, waits for them, and re-layouts  71.1 us (9%)
  matrix products  66 us (8%)
  other arithmetic  65.5 us (8%)
  starting transfers between devices  22.4 us (3%)
  between operations  16.5 us (2%)
    reduce_scatter x1, waiting for transfers between devices, per_device(): lax.psum_scatter(g_w_in, 'fsdp', scatter_dimension=0, tiled=True)  166 us
    all_gather x1, waiting for transfers between devices, per_device(): lax.all_gather(in_columns, 'fsdp', axis=0, tiled=True)  92.8 us
    unnamed x1, blocking collectives  70.2 us
    reduce_scatter x1, waiting for transfers between devices, per_device(): lax.psum_scatter(g_w_out, 'fsdp', scatter_dimension=0, tiled=True)  64.6 us
    psum x1, blocking collectives, per_device(): lax.psum((g_norm, g_conv_w, g_conv_b, shift_full, rate_full, skip_full, g...  39.7 us
    all_gather x1, waiting for transfers between devices, per_device(): lax.all_gather(w_in, 'seq', axis=1, tiled=True)  34.2 us
    unnamed x221, local copies, waits for them, and re-layouts  21.2 us
    dynamic_update_slice x16, local copies, waits for them, and re-layouts, state_space(): lax.scan(advance, jnp.zeros((channels, b_rows.shape[1]), signal.dtype), (...  19.9 us
  transfers between devices with their start and end apart: 15, of which 9 were waited for; matrix products, arithmetic and copies ran while one was open for 24% of the time, Pallas kernels for 0%

commit v1 on v0

--- a/solution.py
+++ b/solution.py
@@ -2,6 +2,7 @@
 import jax.numpy as jnp
 from jax import lax
 from jax.sharding import PartitionSpec as P
+from jax.lax import axis_index, axis_size, ppermute
 
 DI = 2048
 HEADS = 32
@@ -121,8 +122,33 @@
         lax.all_gather(w_in, "seq", axis=1, tiled=True),
         lax.all_gather(w_out, "seq", axis=1, tiled=True),
     )
+
+    def edges_see(x_local, named_axis):
+        z2 = axis_size(named_axis)
+        outcome_arr, answer, work_now = (z2, axis_index(named_axis), x_local.shape[0])
+        now, long_array = (x_local, 1)
+        while long_array < outcome_arr:
+            now = jnp.concatenate(
+                [
+                    now,
+                    ppermute(
+                        now,
+                        named_axis,
+                        tuple(
+                            (
+                                (src_i, (src_i - long_array) % outcome_arr)
+                                for src_i in range(outcome_arr)
+                            )
+                        ),
+                    ),
+                ],
+                0,
+            )
+            long_array = 2 * long_array
+        return jnp.roll(now, answer * work_now, 0)
+
     w_in_full, w_out_full = (
-        lax.all_gather(in_columns, "fsdp", axis=0, tiled=True),
+        edges_see(in_columns, "fsdp"),
         lax.all_gather(out_columns, "fsdp", axis=0, tiled=True),
     )
     normed, norm_pull = jax.vjp(rms_apply, residual, norm_gain)

time: 830 us -> 898 us (1.082)
  waiting for transfers between devices: 425 us -> 496 us
    ppermute x0 -> x2, waiting for transfers between devices: none -> 154 us  [edges_see(): ppermute(now, named_axis, tuple(((src_i, (src_i - long_array) % outcome_a...]
    all_gather x1 -> x0, waiting for transfers between devices: 92.8 us -> none  [per_device(): lax.all_gather(in_columns, 'fsdp', axis=0, tiled=True)]
    unnamed x221 -> x232, local copies, waits for them, and re-layouts: 21.2 us -> 26.2 us
  transfers between devices with their start and end apart: 15 -> 16, of which waited for: 9 -> 10; matrix products, arithmetic and copies ran while one was open for 24% -> 20% of each run, Pallas kernels for 0% -> 0%
where the time goes in v1:
time: 898 us; the launch traced here: 889 us
  waiting for transfers between devices  496 us (55%)
  blocking collectives  156 us (17%)
  other arithmetic  68 us (8%)
  local copies, waits for them, and re-layouts  63.9 us (7%)
  matrix products  61.7 us (7%)
  starting transfers between devices  25.6 us (3%)
  between operations  17 us (2%)
    reduce_scatter x1, waiting for transfers between devices, per_device(): lax.psum_scatter(g_w_in, 'fsdp', scatter_dimension=0, tiled=True)  166 us
    ppermute x2, waiting for transfers between devices, edges_see(): ppermute(now, named_axis, tuple(((src_i, (src_i - long_array) % outcome_a...  154 us
    unnamed x1, blocking collectives  70.2 us
    reduce_scatter x1, waiting for transfers between devices, per_device(): lax.psum_scatter(g_w_out, 'fsdp', scatter_dimension=0, tiled=True)  64.8 us
    psum x1, blocking collectives, per_device(): lax.psum((g_norm, g_conv_w, g_conv_b, shift_full, rate_full, skip_full, g...  39.7 us
    all_gather x1, waiting for transfers between devices, per_device(): lax.all_gather(w_in, 'seq', axis=1, tiled=True)  34.9 us
    unnamed x232, local copies, waits for them, and re-layouts  26.2 us
    all_gather x1, waiting for transfers between devices, per_device(): lax.all_gather(w_out, 'seq', axis=1, tiled=True)  22.2 us
  transfers between devices with their start and end apart: 16, of which 10 were waited for; matrix products, arithmetic and copies ran while one was open for 20% of the time, Pallas kernels for 0%

profile of v1, /device:TPU:0, one launch (start us, length us, event | category | flops | bytes accessed | tf_op | source)
XLA Modules:
  0.0 888.9 jit_solution(8210799760071093894)
XLA Ops:
  8.0 34.9 %all-gather.9.cloned.1.call-done = bf16[8,548,256]{2,1,0:T(8,128)(2,1)} async-done(((bf16[1,548,256]{2,1,0:T(8,128)(2,1)}), bf16[8,548,256]{2,1,0:T(8,128)(2,1)}) %all-gather.9.cloned.1.call-update) | async-done | bytes 2244624 | tf_op jit(solution)/shard_map/all_gather | solution.py:122
  48.0 48.5 %collective-permute-done = bf16[256,4384]{0,1:T(8,128)(2,1)S(1)} collective-permute-done((bf16[256,4384]{0,1:T(8,128)(2,1)S(1)}, bf16[256,4384]{0,1:T(8,128)(2,1)S(1)}, u32[]{:S(2)}, u32[]{:S(2)}) %collective-permute-start) | collective-permute-done | bytes 2244640 | tf_op jit(solution)/shard_map/ppermute | solution.py:134
  102.2 22.2 %all-gather.5.cloned.1.call-done = bf16[512,1024]{1,0:T(8,128)(2,1)} async-done(((bf16[512,128]{1,0:T(8,128)(2,1)}), bf16[512,1024]{1,0:T(8,128)(2,1)}) %all-gather.5.cloned.1.call-update) | async-done | bytes 1048592 | tf_op jit(solution)/shard_map/all_gather | solution.py:123
  126.3 105.1 %collective-permute-done.1 = bf16[512,4384]{0,1:T(8,128)(2,1)} collective-permute-done((bf16[512,4384]{0,1:T(8,128)(2,1)}, bf16[512,4384]{0,1:T(8,128)(2,1)}, u32[]{:S(2)}, u32[]{:S(2)}) %collective-permute-start.1) | collective-permute-done | bytes 4489248 | tf_op jit(solution)/shard_map/ppermute | solution.py:134
  245.5 13.1 %all_gather.16 = bf16[1024,128]{0,1:T(8,128)(2,1)S(1)} all-gather(bf16[128,128]{0,1:T(8,128)(2,1)S(1)} %get-tuple-element.339), channel_id=1, replica_groups=mesh['fsdp'=4,'seq'=8] {'seq'}, dimensions={0}, use_global_device_ids=true | all-gather | bytes 294912 | tf_op jit(solution)/shard_map/all_gather | solution.py:168
  258.6 13.1 %all_gather.17 = bf16[1024,128]{0,1:T(8,128)(2,1)S(1)} all-gather(bf16[128,128]{0,1:T(8,128)(2,1)S(1)} %get-tuple-element.340), channel_id=1, replica_groups=mesh['fsdp'=4,'seq'=8] {'seq'}, dimensions={0}, use_global_device_ids=true | all-gather | bytes 294912 | tf_op jit(solution)/shard_map/all_gather | solution.py:167
  281.0 5.3 all-to-all-start.1
  290.2 11.4 %all-to-all-done.1 = bf16[128,32,64]{0,2,1:T(8,128)(2,1)} async-done(((bf16[128,32,64]{0,2,1:T(8,128)(2,1)}), bf16[128,32,64]{0,2,1:T(8,128)(2,1)}, u32[]{:S(2)}, u32[]{:S(2)}) %all-to-all-start.1) | async-done | bytes 524320 | tf_op jit(solution)/shard_map/all_to_all | solution.py:163
  307.3 12.4 %while.34 = (s32[]{:T(128)}, f32[4,64,128]{2,1,0:T(8,128)S(1)}, f32[8,4,64,128]{3,2,1,0:T(8,128)S(1)}, f32[8,4,1,1]{1,3,2,0:T(1,128)}, f32[8,4]{1,0:T(8,128)S(1)...) while((s32[]{:T(128)}, f32[4,64,128]{2,1,0:T(8,128)S(1)}, ...), condition=%wide.region_3.4_spmd.clone, body=%wide.region_2.3_spmd.clone.sunk | while | flops 131075 | bytes 656556 | solution.py:62
  329.5 19.8 %all_to_all.83 = bf16[8,2,16384]{2,1,0:T(2,128)(2,1)} all-to-all(bf16[8,2,16384]{2,1,0:T(2,128)(2,1)} %reshape.324), channel_id=1, replica_groups=mesh['fsdp'=4,'seq'=8] {'seq'}, dimensions={0} | all-to-all | bytes 1048576 | tf_op jit(solution)/shard_map/all_to_all | solution.py:206
  369.0 15.3 %all-to-all-done.3 = bf16[128,32,64]{0,2,1:T(8,128)(2,1)} async-done(((bf16[128,32,64]{0,2,1:T(8,128)(2,1)}), bf16[128,32,64]{0,2,1:T(8,128)(2,1)}, u32[]{:S(2)}, u32[]{:S(2)}) %all-to-all-start.3) | async-done | bytes 524320 | tf_op jit(solution)/shard_map/all_to_all | solution.py:219
  393.7 33.2 %while.35 = (s32[]{:T(128)}, f32[4,64,128]{2,1,0:T(8,128)S(1)}, f32[8,4]{1,0:T(8,128)}, f32[8,4,64,128]{3,2,1,0:T(8,128)}, f32[8,4,64,128]{3,2,1,0:T(8,128)}, /*...) while((s32[]{:T(128)}, f32[4,64,128]{2,1,0:T(8,128)S(1)}, ...), condition=%wide.region_8.9_spmd.clone, body=%wide.region_6.8_spmd.clone.sunk | while | flops 196608 | bytes 786668 | solution.py:62
  427.0 6.0 fusion.25
  443.5 5.5 multiply_reduce_fusion.10
  453.6 5.6 fusion.77
  473.5 5.0 reduce_window_sum.23
  479.3 9.1 %all-to-all-done.4 = bf16[8,2,16384]{2,1,0:T(2,128)(2,1)S(1)} async-done(((bf16[8,2,16384]{2,1,0:T(2,128)(2,1)}), bf16[8,2,16384]{2,1,0:T(2,128)(2,1)S(1)}, u32[]{:S(2)}, u32[]{:S(2)}) %all-to-all-start.4) | async-done | bytes 524320 | tf_op jit(solution)/shard_map/all_to_all | solution.py:229
  496.2 17.7 %reduce-scatter.10.cloned.1.call-done = f32[128,128]{0,1:T(8,128)} async-done(((f32[1024,128]{0,1:T(8,128)}), f32[128,128]{0,1:T(8,128)}) %reduce-scatter.10.cloned.1.call-update) | async-done | bytes 65552 | tf_op jit(solution)/shard_map/reduce_scatter | solution.py:234
  514.8 9.2 %fusion.101 = f32[1024,4384]{0,1:T(8,128)} fusion(bf16[128,4384]{0,1:T(8,128)(2,1)S(1)} %constant_dynamic-update-slice_fusion.7, f32[1,128,1024]{2,1,0:T(8,128)S(1)} %copy-done.3, f32[1024]{0:T(1024)S(1)} %copy-done.45, f32[128]{0:T(128)S(1)} %copy-done.81), kind=kOutput, calls=%fused_computation.254 | convolution fusion | flops 1149632512 | bytes 19608064 | tf_op jit(solution)/shard_map/dot_general | solution.py:94
  531.3 5.3 multiply_reduce_fusion.16
  536.6 64.8 %reduce-scatter.14.cloned.1.call-done = f32[512,1024]{1,0:T(8,128)} async-done(((f32[2048,1024]{1,0:T(8,128)}), f32[512,1024]{1,0:T(8,128)}) %reduce-scatter.14.cloned.1.call-update) | async-done | bytes 2097168 | tf_op jit(solution)/shard_map/reduce_scatter | solution.py:252
  601.5 166.5 %reduce-scatter.12.cloned.1.call-done = f32[256,4384]{0,1:T(8,128)} async-done(((f32[1024,4384]{0,1:T(8,128)}), f32[256,4384]{0,1:T(8,128)}) %reduce-scatter.12.cloned.1.call-update) | async-done | bytes 4489232 | tf_op jit(solution)/shard_map/reduce_scatter | solution.py:251
  767.9 70.2 %fusion = f32[256,552]{0,1:T(8,128)S(1)} fusion(f32[256,4384]{0,1:T(8,128)} %reduce-scatter.12.cloned.1.call-done), kind=kCustom, calls=%all-reduce-scatter | all-reduce-scatter fusion | flops 1130497 | bytes 5054976
  840.5 39.7 %all-reduce.31 = (f32[1024]{0:T(1024)}, f32[4,2304]{1,0:T(4,128)}, f32[2304]{0:T(1024)}, f32[32]{0:T(128)}, f32[32]{0:T(128)}, /*index=5*/f32[32]{0:T(128)}, f32[2048]{0:T(1024)}) all-reduce(f32[1024]{0:T(1024)S(1)} %get-tuple-element.282, f32[4,2304]{1,0:T(4,128)S(1)} %pad_maximum_fusion.1, ...), channel_id=1, replica_groups=mesh['fsdp'=4,'seq'=8] {'fsdp','seq'}, use_global_device_ids=true, to_apply=%region_21.22 | all-reduce | flops 14688 | bytes 117504 | tf_op jit(solution)/shard_map/psum | solution.py:275
  (431 shorter events, 178.1 us)
Async XLA Ops:
  7.2 35.7 %all-gather.9.cloned.1.call-start = ((), (), s32[]{:S(2)}) async-start(), calls=%async_computation.18 | async-start | bytes 2543616 | tf_op jit(solution)/shard_map/all_gather | solution.py:122
  7.9 116.4 %all-gather.5.cloned.1.call-start = ((), (), s32[]{:S(2)}) async-start(), calls=%async_computation.11 | async-start | bytes 1179648 | tf_op jit(solution)/shard_map/all_gather | solution.py:123
  45.6 51.0 %collective-permute-start = (bf16[256,4384]{0,1:T(8,128)(2,1)S(1)}, bf16[256,4384]{0,1:T(8,128)(2,1)S(1)}, u32[]{:S(2)}, u32[]{:S(2)}) collective-permute-start(bf16[256,4384]{0,1:T(8,128)(2,1)S(1)} %bitcast.435), channel_id=1, source_target_pairs={{0,24},{8,0},{16,8},{24,16},{1,25},{9,1},{17,9},{25,17},{2,26},{10... | collective-permute-start | bytes 6733832 | tf_op jit(solution)/shard_map/ppermute | solution.py:134
  99.3 132.2 %collective-permute-start.1 = (bf16[512,4384]{0,1:T(8,128)(2,1)}, bf16[512,4384]{0,1:T(8,128)(2,1)}, u32[]{:S(2)}, u32[]{:S(2)}) collective-permute-start(bf16[512,4384]{0,1:T(8,128)(2,1)} %pad_maximum_fusion), channel_id=1, source_target_pairs={{0,16},{8,24},{16,0},{24,8},{1,17},{9,25},{17,1},{25,9},{2,18},{10... | collective-permute-start | bytes 13467656 | tf_op jit(solution)/shard_map/ppermute | solution.py:134
  100.8 256.8 %all-gather.7.cloned.1.call-start = ((), (), s32[]{:S(2)}) async-start(), calls=%async_computation.12 | async-start | bytes 5242880 | tf_op jit(solution)/shard_map/all_gather | solution.py:152
  101.1 187.4 %copy-start.82 = (f32[4]{0:T(128)}, f32[4]{0:T(128)S(1)}, u32[]{:S(2)}) copy-start(f32[4]{0:T(128)S(1)} %dynamic_slice.57) | copy-start | bytes 52
  101.2 224.1 %copy-start.96 = (f32[4]{0:T(128)}, f32[4]{0:T(128)S(1)}, u32[]{:S(2)}) copy-start(f32[4]{0:T(128)S(1)} %dynamic_slice.60) | copy-start | bytes 52
  101.3 201.5 %copy-start.48 = (f32[4,64]{1,0:T(4,128)}, f32[4,64]{1,0:T(4,128)S(1)}, u32[]{:S(2)}) copy-start(f32[4,64]{1,0:T(4,128)S(1)} %get-tuple-element.358) | copy-start | bytes 3076
  101.3 201.5 %copy-start.50 = (f32[4,64]{1,0:T(4,128)}, f32[4,64]{1,0:T(4,128)S(1)}, u32[]{:S(2)}) copy-start(f32[4,64]{1,0:T(4,128)S(1)} %get-tuple-element.359) | copy-start | bytes 3076
  101.3 201.5 %copy-start.52 = (f32[4,64]{1,0:T(4,128)}, f32[4,64]{1,0:T(4,128)S(1)}, u32[]{:S(2)}) copy-start(f32[4,64]{1,0:T(4,128)S(1)} %get-tuple-element.360) | copy-start | bytes 3076
  101.3 201.5 %copy-start.54 = (f32[4,64]{1,0:T(4,128)}, f32[4,64]{1,0:T(4,128)S(1)}, u32[]{:S(2)}) copy-start(f32[4,64]{1,0:T(4,128)S(1)} %get-tuple-element.361) | copy-start | bytes 3076
  101.4 219.3 %copy-start.59 = (pred[128,128]{1,0:T(8,128)(4,1)}, pred[128,128]{1,0:T(8,128)(4,1)S(1)}, u32[]{:S(2)}) copy-start(pred[128,128]{1,0:T(8,128)(4,1)S(1)} %iota_compare_fusion) | copy-start | bytes 49156
  271.8 9.1 %all-to-all-start = ((bf16[128,8,4]{0,2,1:T(4,128)(2,1)}), bf16[128,8,4]{0,2,1:T(4,128)(2,1)S(1)}, u32[]{:S(2)}, u32[]{:S(2)}) async-start(bf16[128,8,4]{0,2,1:T(4,128)(2,1)} %bitcast.12), calls=%async_computation | async-start | bytes 16384 | tf_op jit(solution)/shard_map/all_to_all | solution.py:164
  281.0 20.7 %all-to-all-start.1 = ((bf16[128,32,64]{0,2,1:T(8,128)(2,1)}), bf16[128,32,64]{0,2,1:T(8,128)(2,1)}, u32[]{:S(2)}, u32[]{:S(2)}) async-start(bf16[128,32,64]{0,2,1:T(8,128)(2,1)} %bitcast.445), calls=%async_computation.1 | async-start | bytes 1048576 | tf_op jit(solution)/shard_map/all_to_all | solution.py:163
  364.8 19.5 %all-to-all-start.3 = ((bf16[128,32,64]{0,2,1:T(8,128)(2,1)}), bf16[128,32,64]{0,2,1:T(8,128)(2,1)}, u32[]{:S(2)}, u32[]{:S(2)}) async-start(bf16[128,32,64]{0,2,1:T(8,128)(2,1)} %bitcast.448), calls=%async_computation.3 | async-start | bytes 1048576 | tf_op jit(solution)/shard_map/all_to_all | solution.py:219
  368.9 126.5 %reduce-scatter.8.cloned.1.call-start = ((), (), s32[]{:S(2)}) async-start(), calls=%async_computation.13 | async-start | bytes 589824 | tf_op jit(solution)/shard_map/reduce_scatter | solution.py:233
  450.6 63.3 %reduce-scatter.10.cloned.1.call-start = ((), (), s32[]{:S(2)}) async-start(), calls=%async_computation.14 | async-start | bytes 589824 | tf_op jit(solution)/shard_map/reduce_scatter | solution.py:234
  453.3 148.2 %reduce-scatter.14.cloned.1.call-start = ((), (), s32[]{:S(2)}) async-start(), calls=%async_computation.16 | async-start | bytes 10485760 | tf_op jit(solution)/shard_map/reduce_scatter | solution.py:252
  469.3 19.1 %all-to-all-start.4 = ((bf16[8,2,16384]{2,1,0:T(2,128)(2,1)}), bf16[8,2,16384]{2,1,0:T(2,128)(2,1)S(1)}, u32[]{:S(2)}, u32[]{:S(2)}) async-start(bf16[8,2,16384]{2,1,0:T(2,128)(2,1)} %reshape.326), calls=%async_computation.4 | async-start | bytes 1048576 | tf_op jit(solution)/shard_map/all_to_all | solution.py:229
  488.4 26.4 %all-to-all-start.5 = ((bf16[8,128,4]{1,2,0:T(4,128)(2,1)}), bf16[8,128,4]{1,2,0:T(4,128)(2,1)S(1)}, u32[]{:S(2)}, u32[]{:S(2)}) async-start(bf16[8,128,4]{1,2,0:T(4,128)(2,1)} %bitcast.387), calls=%async_computation.7 | async-start | bytes 16384 | tf_op jit(solution)/shard_map/all_to_all | solution.py:230
  491.8 276.1 %reduce-scatter.12.cloned.1.call-start = ((), (), s32[]{:S(2)}) async-start(), calls=%async_computation.15 | async-start | bytes 22446080 | tf_op jit(solution)/shard_map/reduce_scatter | solution.py:251
  524.1 357.6 %reduce-scatter.16.cloned.1.call-start = ((), (), s32[]{:S(2)}) async-start(), calls=%async_computation.17 | async-start | bytes 2359296 | tf_op jit(solution)/shard_map/reduce_scatter | solution.py:256
  601.5 238.0 %copy-start.17 = (f32[1,128,1024]{2,1,0:T(8,128)S(1)}, f32[1,128,1024]{2,1,0:T(8,128)}, u32[]{:S(2)}) copy-start(f32[1,128,1024]{2,1,0:T(8,128)} %param.25) | copy-start | bytes 1572868
  838.2 42.0 %collective-permute-start.2 = (f32[256,28]{0,1:T(8,128)S(1)}, f32[256,28]{0,1:T(8,128)S(1)}, u32[]{:S(2)}, u32[]{:S(2)}) collective-permute-start(f32[256,28]{0,1:T(8,128)S(1)} %slice.156), channel_id=1, source_target_pairs={{0,1},{1,2},{2,3},{3,4},{4,5},{5,6},{6,7},{8,9},{9,10},{10,11},{11... | collective-permute-start | bytes 86024
  (99 other events, 2761.0 us)
Sparse Core Ops, SparseCore 0:
  9.6 33.2 all-gather.8
  100.9 23.4 all-gather.4
  126.2 85.0 all-gather.6
  450.7 31.5 reduce-scatter.7
  484.4 29.4 reduce-scatter.9
  516.9 84.5 reduce-scatter.13
  604.6 163.2 reduce-scatter.11
  770.8 50.0 reduce-scatter.15
